TPU v7x, 32 devices: a whole 2x2x4 slice. The times are simulated.
32 devices in a mesh: wide: 8 (over z, core), col: 4 (over y, x).
Axes of the slice: x: 2, y: 2, z: 4, core: 2. Of those that a mesh axis runs over, the one named last changes fastest.
Arguments:
- amplitudes: float32 [2048, 2048], P('wide', 'col'), may hold values from -6 to 6
- integrals: float32 [2048, 2048], P('wide', 'col'), may hold values from -0.125 to 0.125
Outputs:
- ladder: float32 [2048, 2048], P(('wide', 'col'))
All inputs are finite; a program needn't handle non-finite values.
Results may differ from a plain program's by a relative error of at most 0.00007.
Values sent between devices are 32-bit elements; how exact they have to be, the bound alone decides.
A program may use at most 64 MiB of HBM per device.

v0:
```python
import jax
import jax.numpy as jnp
from jax import lax
from jax.sharding import PartitionSpec as P


def on_device(amplitudes, integrals):
    panel = lax.all_gather(integrals, "wide", axis=0, tiled=True)
    part = lax.dot_general(
        amplitudes,
        panel,
        (((1,), (1,)), ((), ())),
        precision=lax.Precision.HIGHEST,
        preferred_element_type=jnp.float32,
    )
    return lax.psum_scatter(part, "col", scatter_dimension=0, tiled=True)


def solution(mesh):
    return jax.shard_map(
        on_device,
        mesh=mesh,
        in_specs=(P("wide", "col"), P("wide", "col")),
        out_specs=P(("wide", "col"), None),
        check_vma=False,
    )
```

profile of v0, /device:TPU:0, one launch (start us, length us, event | category | flops | bytes accessed | tf_op | source)
XLA Modules:
  0.0 106.9 jit_solution(4373981538191259689)
XLA Ops:
  6.5 0.0 copy-start
  6.5 0.0 all-gather.2.cloned.1.call-start
  6.5 0.7 all-gather.2.cloned.1.call-update
  7.3 0.0 reduce-scatter.2.cloned.1.call-start
  7.3 51.5 %all-gather.2.cloned.1.call-done = f32[2048,512]{1,0:T(8,128)} async-done(((f32[256,512]{1,0:T(8,128)}), f32[2048,512]{1,0:T(8,128)}) %all-gather.2.cloned.1.call-update) | async-done | bytes 4194320 | tf_op jit(solution)/shard_map/all_gather | solution.py:8
  58.8 0.0 copy-done
  58.8 7.1 %fusion = f32[256,2048]{1,0:T(8,128)} fusion(f32[256,512]{1,0:T(8,128)S(1)} %copy-done, f32[2048,512]{1,0:T(8,128)} %all-gather.2.cloned.1.call-done), kind=kOutput, calls=%fused_computation | convolution fusion | flops 3221225472 | bytes 6815744 | tf_op jit(solution)/shard_map/dot_general | solution.py:9
  66.0 0.0 reduce-scatter.2.cloned.1.call-update
  66.0 34.1 %reduce-scatter.2.cloned.1.call-done = f32[64,2048]{1,0:T(8,128)} async-done(((f32[256,2048]{1,0:T(8,128)}), f32[64,2048]{1,0:T(8,128)}) %reduce-scatter.2.cloned.1.call-update) | async-done | bytes 524304 | tf_op jit(solution)/shard_map/reduce_scatter | solution.py:16
Async XLA Ops:
  6.5 52.3 %copy-start = (f32[256,512]{1,0:T(8,128)S(1)}, f32[256,512]{1,0:T(8,128)}, u32[]{:S(2)}) copy-start(f32[256,512]{1,0:T(8,128)} %param.2) | copy-start | bytes 1572868
  6.5 52.3 %all-gather.2.cloned.1.call-start = ((), (), s32[]{:S(2)}) async-start(), calls=%async_computation.1 | async-start | bytes 4718592 | tf_op jit(solution)/shard_map/all_gather | solution.py:8
  7.3 92.8 %reduce-scatter.2.cloned.1.call-start = ((), (), s32[]{:S(2)}) async-start(), calls=%async_computation.2 | async-start | bytes 2621440 | tf_op jit(solution)/shard_map/reduce_scatter | solution.py:16
Sparse Core Ops, SparseCore 0:
  9.0 49.8 all-gather.1
  66.1 33.9 reduce-scatter.1
where the time goes:
time: 107 us
  waiting for transfers between devices  86.3 us (81%)
  between operations  13.4 us (13%)
  matrix products  7.14 us (7%)
    all_gather x1, waiting for transfers between devices, on_device(): panel = lax.all_gather(integrals, 'wide', axis=0, tiled=True)  51.5 us
    reduce_scatter x1, waiting for transfers between devices, on_device(): return lax.psum_scatter(part, 'col', scatter_dimension=0, tiled=True)  34.1 us
    dot_general x1, matrix products, on_device(): lax.dot_general(amplitudes, panel, (((1,), (1,)), ((), ())), precision=la...  7.14 us
  transfers between devices with their start and end apart: 2, of which 2 were waited for; matrix products, arithmetic and copies ran while one was open for 0% of the time, Pallas kernels for 0%

commit v1 on v0

--- a/solution.py
+++ b/solution.py
@@ -4,8 +4,25 @@
 from jax.sharding import PartitionSpec as P
 
 
+def laid_out(blocks, dim):
+    lengths = list(blocks.shape[1:])
+    lengths[dim] *= blocks.shape[0]
+    return jnp.moveaxis(blocks, 0, dim).reshape(lengths)
+
+
+def gather_around(array, axis, dim):
+    devices = lax.axis_size(axis)
+    right = [(i, (i + 1) % devices) for i in range(devices)]
+    blocks = [array]
+    while len(blocks) < devices:
+        blocks.append(lax.ppermute(blocks[-1], axis, right))
+    position = lax.axis_index(axis)
+    blocks = jnp.stack(blocks)[(position - jnp.arange(devices)) % devices]
+    return laid_out(blocks, dim)
+
+
 def on_device(amplitudes, integrals):
-    panel = lax.all_gather(integrals, "wide", axis=0, tiled=True)
+    panel = gather_around(integrals, "wide", 0)
     part = lax.dot_general(
         amplitudes,
         panel,

time: 107 us -> 135 us (1.26)
  waiting for transfers between devices: 86.3 us -> 101 us
  local copies, waits for them, and re-layouts: 0.01 us -> 14.6 us
  matrix products: 7.14 us -> 5.28 us
    ppermute x0 -> x7, waiting for transfers between devices: none -> 66.6 us  [gather_around(): blocks.append(lax.ppermute(blocks[-1], axis, right))]
    all_gather x1 -> x0, waiting for transfers between devices: 51.5 us -> none  [on_device(): panel = lax.all_gather(integrals, 'wide', axis=0, tiled=True)]
    unnamed x2 -> x10, local copies, waits for them, and re-layouts: 0.01 us -> 8.78 us
    gather x0 -> x1, local copies, waits for them, and re-layouts: none -> 4.98 us  [gather_around(): blocks = jnp.stack(blocks)[(position - jnp.arange(devices)) % devices]]
    dot_general x1, matrix products: 7.14 us -> 5.28 us  [on_device(): lax.dot_general(amplitudes, panel, (((1,), (1,)), ((), ())), precision=la...]
  transfers between devices with their start and end apart: 2 -> 8, of which waited for: 2 -> 8; matrix products, arithmetic and copies ran while one was open for 0% -> 5% of each run, Pallas kernels for 0% -> 0%
where the time goes in v1:
time: 135 us; the launch traced here: 134 us
  waiting for transfers between devices  101 us (75%)
  local copies, waits for them, and re-layouts  14.6 us (11%)
  between operations  13.4 us (10%)
  matrix products  5.28 us (4%)
    ppermute x7, waiting for transfers between devices, gather_around(): blocks.append(lax.ppermute(blocks[-1], axis, right))  66.6 us
    reduce_scatter x1, waiting for transfers between devices, on_device(): return lax.psum_scatter(part, 'col', scatter_dimension=0, tiled=True)  34 us
    unnamed x10, local copies, waits for them, and re-layouts  8.78 us
    dot_general x1, matrix products, on_device(): lax.dot_general(amplitudes, panel, (((1,), (1,)), ((), ())), precision=la...  5.28 us
    gather x1, local copies, waits for them, and re-layouts, gather_around(): blocks = jnp.stack(blocks)[(position - jnp.arange(devices)) % devices]  4.98 us
  transfers between devices with their start and end apart: 8, of which 8 were waited for; matrix products, arithmetic and copies ran while one was open for 5% of the time, Pallas kernels for 0%

profile of v1, /device:TPU:0, one launch (start us, length us, event | category | flops | bytes accessed | tf_op | source)
XLA Modules:
  0.0 134.4 jit_solution(9763086837142303598)
XLA Ops:
  6.5 0.0 copy-start
  6.5 0.0 reduce-scatter.4.cloned.1.call-start
  6.5 0.5 collective-permute-start
  7.0 11.1 %collective-permute-done = f32[256,512]{1,0:T(8,128)S(1)} collective-permute-done((f32[256,512]{1,0:T(8,128)}, f32[256,512]{1,0:T(8,128)S(1)}, u32[]{:S(2)}, u32[]{:S(2)}) %collective-permute-start) | collective-permute-done | bytes 524320 | tf_op jit(solution)/shard_map/ppermute | solution.py:18
  18.1 0.0 collective-permute-start.1
  18.1 10.4 %collective-permute-done.1 = f32[256,512]{1,0:T(8,128)S(1)} collective-permute-done((f32[256,512]{1,0:T(8,128)S(1)}, f32[256,512]{1,0:T(8,128)S(1)}, u32[]{:S(2)}, u32[]{:S(2)}) %collective-permute-start.1) | collective-permute-done | bytes 524320 | tf_op jit(solution)/shard_map/ppermute | solution.py:18
  28.5 0.0 collective-permute-start.2
  28.5 10.4 %collective-permute-done.2 = f32[256,512]{1,0:T(8,128)S(1)} collective-permute-done((f32[256,512]{1,0:T(8,128)S(1)}, f32[256,512]{1,0:T(8,128)S(1)}, u32[]{:S(2)}, u32[]{:S(2)}) %collective-permute-start.2) | collective-permute-done | bytes 524320 | tf_op jit(solution)/shard_map/ppermute | solution.py:18
  38.9 0.0 collective-permute-start.3
  38.9 10.4 %collective-permute-done.3 = f32[256,512]{1,0:T(8,128)S(1)} collective-permute-done((f32[256,512]{1,0:T(8,128)S(1)}, f32[256,512]{1,0:T(8,128)S(1)}, u32[]{:S(2)}, u32[]{:S(2)}) %collective-permute-start.3) | collective-permute-done | bytes 524320 | tf_op jit(solution)/shard_map/ppermute | solution.py:18
  49.3 0.0 collective-permute-start.4
  49.3 1.9 %bitcast_dynamic-update-slice_fusion.7 = f32[8,256,512]{2,1,0:T(8,128)} fusion(f32[256,512]{1,0:T(8,128)} %param.3), kind=kLoop, calls=%fused_computation.9 | loop fusion | bytes 1048576
  51.2 8.5 %collective-permute-done.4 = f32[256,512]{1,0:T(8,128)S(1)} collective-permute-done((f32[256,512]{1,0:T(8,128)S(1)}, f32[256,512]{1,0:T(8,128)S(1)}, u32[]{:S(2)}, u32[]{:S(2)}) %collective-permute-start.4) | collective-permute-done | bytes 524320 | tf_op jit(solution)/shard_map/ppermute | solution.py:18
  59.7 0.0 collective-permute-start.5
  59.7 0.8 bitcast_dynamic-update-slice_fusion.6
  60.6 0.8 bitcast_dynamic-update-slice_fusion.5
  61.4 0.8 bitcast_dynamic-update-slice_fusion.4
  62.2 7.9 %collective-permute-done.5 = f32[256,512]{1,0:T(8,128)S(1)} collective-permute-done((f32[256,512]{1,0:T(8,128)S(1)}, f32[256,512]{1,0:T(8,128)S(1)}, u32[]{:S(2)}, u32[]{:S(2)}) %collective-permute-start.5) | collective-permute-done | bytes 524320 | tf_op jit(solution)/shard_map/ppermute | solution.py:18
  70.1 0.0 collective-permute-start.6
  70.1 0.8 bitcast_dynamic-update-slice_fusion.3
  71.0 0.8 bitcast_dynamic-update-slice_fusion.2
  71.8 0.8 bitcast_dynamic-update-slice_fusion.1
  72.7 7.9 %collective-permute-done.6 = f32[256,512]{1,0:T(8,128)S(1)} collective-permute-done((f32[256,512]{1,0:T(8,128)S(1)}, f32[256,512]{1,0:T(8,128)S(1)}, u32[]{:S(2)}, u32[]{:S(2)}) %collective-permute-start.6) | collective-permute-done | bytes 524320 | tf_op jit(solution)/shard_map/ppermute | solution.py:18
  80.5 0.8 bitcast_dynamic-update-slice_fusion
  81.4 5.0 %gather_fusion = f32[8,256,512]{2,1,0:T(8,128)} fusion(f32[8,256,512]{2,1,0:T(8,128)} %bitcast_dynamic-update-slice_fusion, s32[1024]{0:T(1024)S(1)} %pad_clamp_fusion), kind=kCustom, calls=%fused_computation | custom fusion | bytes 8388640 | tf_op jit(solution)/shard_map/gather | solution.py:20
  86.3 0.0 copy-done
  86.3 5.3 %convolution_bitcast_fusion = f32[256,2048]{0,1:T(8,128)S(1)} fusion(f32[2048,512]{1,0:T(8,128)} %bitcast.24, f32[256,512]{1,0:T(8,128)S(1)} %copy-done), kind=kOutput, calls=%fused_computation.1 | convolution fusion | flops 3221225472 | bytes 6815744 | tf_op jit(solution)/shard_map/dot_general | solution.py:26
  91.6 1.9 %copy.5 = f32[256,2048]{1,0:T(8,128)} copy(f32[256,2048]{0,1:T(8,128)S(1)} %convolution_bitcast_fusion) | data formatting | bytes 4194304
  93.5 0.0 reduce-scatter.4.cloned.1.call-update
  93.5 34.0 %reduce-scatter.4.cloned.1.call-done = f32[64,2048]{1,0:T(8,128)} async-done(((f32[256,2048]{1,0:T(8,128)}), f32[64,2048]{1,0:T(8,128)}) %reduce-scatter.4.cloned.1.call-update) | async-done | bytes 524304 | tf_op jit(solution)/shard_map/reduce_scatter | solution.py:33
  (2 shorter events, 0.0 us)
Async XLA Ops:
  6.5 79.8 %copy-start = (f32[256,512]{1,0:T(8,128)S(1)}, f32[256,512]{1,0:T(8,128)}, u32[]{:S(2)}) copy-start(f32[256,512]{1,0:T(8,128)} %param.2) | copy-start | bytes 1572868
  6.5 121.0 %reduce-scatter.4.cloned.1.call-start = ((), (), s32[]{:S(2)}) async-start(), calls=%async_computation.1 | async-start | bytes 2621440 | tf_op jit(solution)/shard_map/reduce_scatter | solution.py:33
  6.5 11.6 %collective-permute-start = (f32[256,512]{1,0:T(8,128)}, f32[256,512]{1,0:T(8,128)S(1)}, u32[]{:S(2)}, u32[]{:S(2)}) collective-permute-start(f32[256,512]{1,0:T(8,128)} %param.3), channel_id=1, source_target_pairs={{0,4},{4,8},{8,12},{12,16},{16,20},{20,24},{24,28},{28,0},{1,5},{5... | collective-permute-start | bytes 1572872 | tf_op jit(solution)/shard_map/ppermute | solution.py:18
  18.1 10.4 %collective-permute-start.1 = (f32[256,512]{1,0:T(8,128)S(1)}, f32[256,512]{1,0:T(8,128)S(1)}, u32[]{:S(2)}, u32[]{:S(2)}) collective-permute-start(f32[256,512]{1,0:T(8,128)S(1)} %collective-permute-done), channel_id=1, source_target_pairs={{0,4},{4,8},{8,12},{12,16},{16,20},{20,24},{24,28},{28,0},{1,5},{5... | collective-permute-start | bytes 1572872 | tf_op jit(solution)/shard_map/ppermute | solution.py:18
  28.5 10.4 %collective-permute-start.2 = (f32[256,512]{1,0:T(8,128)S(1)}, f32[256,512]{1,0:T(8,128)S(1)}, u32[]{:S(2)}, u32[]{:S(2)}) collective-permute-start(f32[256,512]{1,0:T(8,128)S(1)} %collective-permute-done.1), channel_id=1, source_target_pairs={{0,4},{4,8},{8,12},{12,16},{16,20},{20,24},{24,28},{28,0},{1,5},{5... | collective-permute-start | bytes 1572872 | tf_op jit(solution)/shard_map/ppermute | solution.py:18
  38.9 10.4 %collective-permute-start.3 = (f32[256,512]{1,0:T(8,128)S(1)}, f32[256,512]{1,0:T(8,128)S(1)}, u32[]{:S(2)}, u32[]{:S(2)}) collective-permute-start(f32[256,512]{1,0:T(8,128)S(1)} %collective-permute-done.2), channel_id=1, source_target_pairs={{0,4},{4,8},{8,12},{12,16},{16,20},{20,24},{24,28},{28,0},{1,5},{5... | collective-permute-start | bytes 1572872 | tf_op jit(solution)/shard_map/ppermute | solution.py:18
  49.3 10.4 %collective-permute-start.4 = (f32[256,512]{1,0:T(8,128)S(1)}, f32[256,512]{1,0:T(8,128)S(1)}, u32[]{:S(2)}, u32[]{:S(2)}) collective-permute-start(f32[256,512]{1,0:T(8,128)S(1)} %collective-permute-done.3), channel_id=1, source_target_pairs={{0,4},{4,8},{8,12},{12,16},{16,20},{20,24},{24,28},{28,0},{1,5},{5... | collective-permute-start | bytes 1572872 | tf_op jit(solution)/shard_map/ppermute | solution.py:18
  59.7 10.4 %collective-permute-start.5 = (f32[256,512]{1,0:T(8,128)S(1)}, f32[256,512]{1,0:T(8,128)S(1)}, u32[]{:S(2)}, u32[]{:S(2)}) collective-permute-start(f32[256,512]{1,0:T(8,128)S(1)} %collective-permute-done.4), channel_id=1, source_target_pairs={{0,4},{4,8},{8,12},{12,16},{16,20},{20,24},{24,28},{28,0},{1,5},{5... | collective-permute-start | bytes 1572872 | tf_op jit(solution)/shard_map/ppermute | solution.py:18
  70.1 10.4 %collective-permute-start.6 = (f32[256,512]{1,0:T(8,128)S(1)}, f32[256,512]{1,0:T(8,128)S(1)}, u32[]{:S(2)}, u32[]{:S(2)}) collective-permute-start(f32[256,512]{1,0:T(8,128)S(1)} %collective-permute-done.5), channel_id=1, source_target_pairs={{0,4},{4,8},{8,12},{12,16},{16,20},{20,24},{24,28},{28,0},{1,5},{5... | collective-permute-start | bytes 1572872 | tf_op jit(solution)/shard_map/ppermute | solution.py:18
Sparse Core Ops, SparseCore 0:
  93.6 33.8 reduce-scatter.3
